TPU v7x, 256 devices: a whole 4x4x8 slice. The times are simulated.
256 devices in a mesh: slab: 128 (over z, y_lo, x, core), plane: 2 (over y_hi).
Axes of the slice: x: 4, y: 4 (y_hi: 2, y_lo: 2; y = y_hi * 2 + y_lo), z: 8, core: 2. Of those that a mesh axis runs over, the one named last changes fastest.
Arguments:
- probe_pos: bfloat16 [3, 32768], P(None, ('slab', 'plane')), may hold values from 0 to 2
- atom_pos: bfloat16 [3, 32768], P(None, ('slab', 'plane')), may hold values from 0 to 2
- atom_feat: bfloat16 [128, 32768], P(None, ('slab', 'plane')), may hold values from -6 to 6
- neighbours: int32 [32, 32768], P(None, ('slab', 'plane')), may hold values from 0 to 32767, as said below
- valid: int32 [32, 32768], P(None, ('slab', 'plane')), may hold values 0 or 1
- w_radial1: float32 [64, 8], replicated, may hold values from -2 to 2
- w_radial2: bfloat16 [640, 64], replicated, may hold values from -0.75 to 0.75
- readout: float32 [5, 128], replicated, may hold values from -0.5 to 0.5
- cotangent: float32 [32768], P(('slab', 'plane')), may hold values from -6 to 6
Outputs:
- density: float32 [32768], P(('slab', 'plane'))
- grad_feat: float32 [128, 32768], P(None, ('slab', 'plane'))
- grad_radial1: float32 [64, 8], replicated
- grad_radial2: float32 [640, 64], replicated
- grad_readout: float32 [5, 128], replicated
Inputs may be any that keep to these rules, and one draw needn't show every extreme that they name: `neighbours`: the atom of every slot of probe p lies in the slab of p (atoms a with a // 256 = p // 256) or in one of the two slabs beside it on the periodic cycle of slabs.
All inputs are finite; a program needn't handle non-finite values. No bound on the sum of `valid` on one device may be relied on, other than what follows from the above.
Results may differ from a plain program's by a relative error of at most 0.0049.
Values may be sent and summed in bfloat16 or wider, within the bound.
No kernel may reach another device: no remote copies, remote signals or barrier semaphores. Data moves between devices by JAX's collectives and lax.ppermute only.
A program may use at most 128 MiB of HBM per device.

v0:
```python
import math
import jax
import jax.numpy as jnp
from jax import lax
from jax.sharding import PartitionSpec as P

slab_width = 2.0
soften = 0.25


def padded(block, sides, width):
    for axis, dim in sides:
        count = lax.axis_size(axis)
        forward = [(i, i + 1) for i in range(count - 1)]
        forward.append((count - 1, 0))
        backward = [(target, source) for source, target in forward]
        low = lax.ppermute(
            lax.slice_in_dim(block, block.shape[dim] - width, None, axis=dim), axis, forward
        )
        high = lax.ppermute(lax.slice_in_dim(block, 0, width, axis=dim), axis, backward)
        block = jnp.concatenate([low, block, high], axis=dim)
    return block


def passed_along(block, axis, distance):
    devices = range(lax.axis_size(axis))
    route = [((i - distance) % len(devices), i) for i in devices]
    return lax.ppermute(block, axis, route)


def harmonics(along_x, along_y, along_z):
    sq_x = along_x * along_x
    sq_y = along_y * along_y
    sq_z = along_z * along_z
    root3 = math.sqrt(3.0)
    root15 = math.sqrt(15.0)
    root5 = math.sqrt(5.0)
    coef_a1 = math.sqrt(35.0 / 8.0)
    coef_a2 = math.sqrt(105.0)
    coef_a3 = math.sqrt(21.0 / 8.0)
    coef_a4 = math.sqrt(7.0) / 2.0
    coef_b1 = 3.0 * math.sqrt(35.0) / 2.0
    coef_b2 = 3.0 * math.sqrt(70.0) / 4.0
    coef_b3 = 3.0 * math.sqrt(5.0) / 2.0
    coef_b4 = 3.0 * math.sqrt(10.0) / 4.0
    rows_out = [
        jnp.ones_like(along_x),
        root3 * along_y,
        root3 * along_z,
        root3 * along_x,
        root15 * along_x * along_y,
        root15 * along_y * along_z,
        root5 / 2.0 * (3.0 * sq_z - 1.0),
        root15 * along_x * along_z,
        root15 / 2.0 * (sq_x - sq_y),
        coef_a1 * along_y * (3.0 * sq_x - sq_y),
        coef_a2 * along_x * along_y * along_z,
        coef_a3 * along_y * (5.0 * sq_z - 1.0),
        coef_a4 * along_z * (5.0 * sq_z - 3.0),
        coef_a3 * along_x * (5.0 * sq_z - 1.0),
        coef_a2 / 2.0 * along_z * (sq_x - sq_y),
        coef_a1 * along_x * (sq_x - 3.0 * sq_y),
        coef_b1 * along_x * along_y * (sq_x - sq_y),
        coef_b2 * along_y * along_z * (3.0 * sq_x - sq_y),
        coef_b3 * along_x * along_y * (7.0 * sq_z - 1.0),
        coef_b4 * along_y * along_z * (7.0 * sq_z - 3.0),
        0.375 * (35.0 * sq_z * sq_z - 30.0 * sq_z + 3.0),
        coef_b4 * along_x * along_z * (7.0 * sq_z - 3.0),
        coef_b3 / 2.0 * (sq_x - sq_y) * (7.0 * sq_z - 1.0),
        coef_b2 * along_x * along_z * (sq_x - 3.0 * sq_y),
        coef_b1 / 4.0 * (sq_x * (sq_x - 3.0 * sq_y) - sq_y * (3.0 * sq_x - sq_y)),
    ]
    return jnp.stack(rows_out)


def probe_block(
    features, atom_xyz, probe_xyz, offset, weight_mask, cot_block, w_radial1, w_radial2, readout
):
    slots, block_len = weight_mask.shape
    edge_count = slots * block_len
    channels = features.shape[0]
    degrees = readout.shape[0]
    probe_tile = jnp.broadcast_to(probe_xyz[:, None, :], (3, slots, block_len)).reshape(
        3, edge_count
    )
    delta_x = atom_xyz[0] - probe_tile[0]
    delta_y = atom_xyz[1] - probe_tile[1]
    delta_z = atom_xyz[2] + slab_width * offset.reshape(edge_count) - probe_tile[2]
    radius = jnp.sqrt(delta_x * delta_x + delta_y * delta_y + delta_z * delta_z + soften)
    sphere = harmonics(delta_x / radius, delta_y / radius, delta_z / radius)
    centres = 0.75 * jnp.arange(w_radial1.shape[1], dtype=jnp.float32)
    radial_basis = jnp.exp(-2.0 * (radius[None, :] - centres[:, None]) ** 2)
    preact = jnp.dot(w_radial1, radial_basis, precision=lax.Precision.HIGHEST)
    hidden = jax.nn.silu(preact).astype(jnp.bfloat16)
    radial = jnp.dot(w_radial2, hidden, preferred_element_type=jnp.float32).reshape(
        degrees, channels, edge_count
    )
    weight = weight_mask.reshape(edge_count) * (1.0 / math.sqrt(slots))
    feat_float = features.astype(jnp.float32)
    messages = (radial * feat_float[None] * weight[None, None, :]).reshape(
        degrees, channels, slots, block_len
    )
    sphere_rows = sphere.reshape(degrees * degrees, slots, block_len)
    density = jnp.zeros((block_len,), jnp.float32)
    grad_msg = []
    grad_read = []
    for degree in range(degrees):
        part_y = sphere_rows[degree * degree : (degree + 1) * (degree + 1)]
        moment = jnp.einsum(
            "kjp,cjp->kcp", part_y, messages[degree], precision=lax.Precision.HIGHEST
        )
        if degree == 0:
            density = jnp.sum(readout[0][:, None] * moment[0], axis=0)
            grad_mom = cot_block[None, None, :] * readout[0][None, :, None]
            grad_read.append(jnp.sum(cot_block[None, :] * moment[0], axis=1))
        else:
            squares = jnp.sum(moment * moment, axis=0)
            density = density + jnp.sum(readout[degree][:, None] * squares, axis=0)
            grad_mom = 2.0 * cot_block[None, None, :] * readout[degree][None, :, None] * moment
            grad_read.append(jnp.sum(cot_block[None, :] * squares, axis=1))
        grad_msg.append(
            jnp.einsum("kjp,kcp->cjp", part_y, grad_mom, precision=lax.Precision.HIGHEST)
        )
    grad_messages = jnp.stack(grad_msg).reshape(degrees, channels, edge_count)
    grad_features = jnp.sum(grad_messages * radial, axis=0) * weight[None, :]
    grad_radial = (
        (grad_messages * feat_float[None] * weight[None, None, :])
        .reshape(degrees * channels, edge_count)
        .astype(jnp.bfloat16)
    )
    grad_w2 = lax.dot_general(
        grad_radial, hidden, (((1,), (1,)), ((), ())), preferred_element_type=jnp.float32
    )
    grad_hidden = lax.dot_general(
        w_radial2, grad_radial, (((0,), (0,)), ((), ())), preferred_element_type=jnp.float32
    )
    logistic = jax.nn.sigmoid(preact)
    grad_pre = grad_hidden * logistic * (1.0 + preact * (1.0 - logistic))
    grad_w1 = lax.dot_general(
        grad_pre, radial_basis, (((1,), (1,)), ((), ())), precision=lax.Precision.HIGHEST
    )
    return (density, grad_features, grad_w1, grad_w2, jnp.stack(grad_read))


def shards(
    probe_pos, atom_pos, atom_feat, neighbours, valid, w_radial1, w_radial2, readout, cotangent
):
    channels = atom_feat.shape[0]
    atom_dev = atom_feat.shape[1]
    plane_count = lax.axis_size("plane")
    slab_count = lax.axis_size("slab")
    slab_index = lax.axis_index("slab")
    atom_slab = atom_dev * plane_count
    atom_pack = jnp.concatenate([atom_feat, atom_pos], axis=0)
    slab_pack = lax.all_gather(atom_pack, "plane", axis=1, tiled=True)
    window = padded(slab_pack, (("slab", 1),), atom_slab)
    window_feat = window[:channels]
    window_xyz = window[channels:]
    local_rows = (neighbours - (slab_index - 1) * atom_slab) % (slab_count * atom_slab)
    offsets = (local_rows // atom_slab - 1).astype(jnp.float32)
    slots, probe_dev = neighbours.shape
    block_len = 128
    count = probe_dev // block_len
    rows_blocks = local_rows.reshape(slots, count, block_len).transpose(1, 0, 2)
    offset_blocks = offsets.reshape(slots, count, block_len).transpose(1, 0, 2)
    mask_blocks = valid.astype(jnp.float32).reshape(slots, count, block_len).transpose(1, 0, 2)
    probe_blocks = probe_pos.astype(jnp.float32).reshape(3, count, block_len).transpose(1, 0, 2)
    cot_blocks = cotangent.reshape(count, block_len)

    def advance(totals, inputs):
        grad_window, total_w1, total_w2, total_read = totals
        atom_rows, offset, mask_float, probe_xyz, cot_block = inputs
        flat_rows = atom_rows.reshape(-1)
        features = jnp.take(window_feat, flat_rows, axis=1)
        atom_xyz = jnp.take(window_xyz, flat_rows, axis=1).astype(jnp.float32)
        density, grad_features, grad_w1, grad_w2, grad_read = probe_block(
            features,
            atom_xyz,
            probe_xyz,
            offset,
            mask_float,
            cot_block,
            w_radial1,
            w_radial2,
            readout,
        )
        grad_window = grad_window.at[:, flat_rows].add(grad_features)
        return (
            (grad_window, total_w1 + grad_w1, total_w2 + grad_w2, total_read + grad_read),
            density,
        )

    start_totals = (
        jnp.zeros((channels, 3 * atom_slab), jnp.float32),
        jnp.zeros(w_radial1.shape, jnp.float32),
        jnp.zeros(w_radial2.shape, jnp.float32),
        jnp.zeros(readout.shape, jnp.float32),
    )
    totals, densities = lax.scan(
        advance, start_totals, (rows_blocks, offset_blocks, mask_blocks, probe_blocks, cot_blocks)
    )
    grad_window = totals[0]
    lower_part = passed_along(grad_window[:, :atom_slab], "slab", -1)
    upper_part = passed_along(grad_window[:, 2 * atom_slab :], "slab", 1)
    owned_part = grad_window[:, atom_slab : 2 * atom_slab] + lower_part + upper_part
    grad_feat = lax.psum_scatter(owned_part, "plane", scatter_dimension=1, tiled=True)
    summed_w1, summed_w2, summed_read = lax.psum(
        (totals[1], totals[2], totals[3]), ("slab", "plane")
    )
    scale = 1.0 / math.sqrt(probe_dev * slab_count * plane_count)
    return (
        densities.reshape(-1),
        grad_feat,
        summed_w1 * scale,
        summed_w2 * scale,
        summed_read * scale,
    )


def solution(mesh):
    in_specs = (
        P(None, ("slab", "plane")),
        P(None, ("slab", "plane")),
        P(None, ("slab", "plane")),
        P(None, ("slab", "plane")),
        P(None, ("slab", "plane")),
        P(),
        P(),
        P(),
        P(("slab", "plane")),
    )
    out_specs = (P(("slab", "plane")), P(None, ("slab", "plane")), P(), P(), P())
    return jax.shard_map(shards, mesh=mesh, in_specs=in_specs, out_specs=out_specs, check_vma=False)
```

profile of v0, /device:TPU:1, one launch (start us, length us, event | category | flops | bytes accessed | tf_op | source)
XLA Modules:
  0.0 536.8 jit_solution(2991363688126804630)
XLA Ops:
  9.8 6.0 %all_gather.3 = bf16[131,256]{0,1:T(8,128)(2,1)S(1)} all-gather(bf16[131,128]{0,1:T(8,128)(2,1)S(1)} %pad_maximum_fusion), channel_id=1, replica_groups=mesh['slab'=128,'plane'=2] {'plane'}, dimensions={1}, use_global_device_ids=true | all-gather | bytes 100608 | tf_op jit(solution)/shard_map/all_gather | solution.py:155
  24.4 12.1 %gather_fusion = bf16[4096,3]{1,0:T(8,128)(2,1)S(1)} fusion(bf16[3,768]{0,1:T(8,128)(2,1)S(1)} %slice.163, s32[4096]{0:T(1024)S(1)} %broadcast_clamp_fusion), kind=kCustom, calls=%fused_computation | custom fusion | bytes 65536 | tf_op jit(solution)/shard_map/while/body/eval_jaxpr/jit(_take)/gather | solution.py:175
  41.3 5.4 %fusion.59 = f32[4096,640]{0,1:T(8,128)} fusion(bf16[640,64]{0,1:T(8,128)(2,1)S(1)} %copy-done, f32[64,4096]{1,0:T(8,128)S(1)} %convolution_bitcast_fusion.1), kind=kOutput, calls=%fused_computation.167 | convolution fusion | flops 336855040 | bytes 11616256 | tf_op jit(solution)/shard_map/while/body/eval_jaxpr/dot_general | solution.py:95
  46.8 11.3 %copy.168 = f32[5,128,4096]{1,2,0:T(8,128)} copy(f32[5,128,4096]{2,1,0:T(8,128)} %bitcast.125) | data formatting | bytes 20971520 | tf_op jit(solution)/shard_map/while/body/eval_jaxpr/reshape | solution.py:95
  58.0 14.9 %gather_fusion.1 = bf16[4096,128]{1,0:T(8,128)(2,1)} fusion(bf16[128,768]{0,1:T(8,128)(2,1)S(1)} %slice.167, s32[4096]{0:T(1024)S(1)} %broadcast_clamp_fusion), kind=kCustom, calls=%fused_computation.1 | custom fusion | bytes 2113536 | tf_op jit(solution)/shard_map/while/body/eval_jaxpr/jit(_take)/gather | solution.py:174
  72.9 3.4 convert_bitcast_fusion
  76.3 5.8 %multiply_multiply_fusion = f32[5,128,4096]{1,2,0:T(8,128)S(1)} fusion(f32[5,128,4096]{1,2,0:T(8,128)} %copy.168, f32[4096]{0:T(1024)S(1)} %multiply_bitcast_fusion.1, f32[128,4096]{0,1:T(8,128)S(1)} %convert_bitcast_fusion), kind=kLoop, calls=%fused_computation.6 | loop fusion | flops 5242880 | bytes 23085056 | tf_op jit(solution)/shard_map/while/body/eval_jaxpr/mul | solution.py:100
  82.1 4.0 fusion.61
  86.1 5.2 fusion.5
  101.6 4.8 multiply_reduce_fusion.1
  106.5 3.1 multiply_reduce_fusion.4
  109.7 3.3 multiply_reduce_fusion.3
  113.1 3.1 multiply_reduce_fusion.2
  116.9 3.5 convolution_bitcast_fusion.5
  121.6 3.9 convolution_bitcast_fusion.4
  126.7 3.5 convolution_bitcast_fusion.3
  131.4 3.5 convolution_bitcast_fusion.2
  139.1 7.6 %broadcast_multiply_fusion = (f32[5,128,4096]{1,2,0:T(8,128)}, f32[128,4096]{0,1:T(8,128)}) fusion(f32[5,128,4096]{1,2,0:T(8,128)S(1)} %constant_dynamic-update-slice_fusion.3, f32[128,4096]{0,1:T(8,128)S(1)} %convert_bitcast_fusion, f32[5,128,4096]{1,2,0:T(8,128)S(1)} %bitcast.124), kind=kLoop, calls=%fused_computation.7 | loop fusion | flops 7340032 | bytes 35651584 | tf_op jit(solution)/shard_map/while/body/eval_jaxpr/mul | solution.py:127
  146.7 11.3 %copy.186 = f32[5,128,4096]{2,1,0:T(8,128)} copy(f32[5,128,4096]{1,2,0:T(8,128)} %get-tuple-element.109) | data formatting | bytes 20971520 | tf_op jit(solution)/shard_map/while/body/eval_jaxpr/mul | solution.py:127
  158.0 5.4 %fusion = bf16[640,4096]{1,0:T(8,128)(2,1)S(1)} fusion(f32[5,128,4096]{2,1,0:T(8,128)} %copy.186, f32[4096]{0:T(1024)S(1)} %multiply_bitcast_fusion.1), kind=kLoop, calls=%fused_computation.4 | loop fusion | flops 5242880 | bytes 15745024 | tf_op jit(solution)/shard_map/while/body/eval_jaxpr/convert_element_type | solution.py:129
  167.9 24.6 %scatter_custom_fusion = f32[128,768]{0,1:T(8,128)S(1)} fusion(s32[4096]{0:T(1024)} %bitcast.154, f32[128,4096]{0,1:T(8,128)S(1)} %copy-done.4, f32[4096]{0:T(1024)S(1)} %multiply_bitcast_fusion.1, f32[]{:T(128)} %constant.170.clone.1), kind=kCustom, calls=%fused_computation.12 | custom fusion | flops 1048576 | bytes 2507264 | tf_op jit(solution)/shard_map/while/body/eval_jaxpr/scatter-add | solution.py:187
  193.7 4.9 collective-permute-start.2
  200.9 80.1 %all-reduce = (f32[64,8]{0,1:T(8,128)S(1)}, f32[5,128]{1,0:T(8,128)S(1)}) all-reduce(f32[64,8]{0,1:T(8,128)S(1)} %fusion.39, f32[5,128]{1,0:T(8,128)S(1)} %stack.121), channel_id=1, replica_groups=mesh['slab'=128,'plane'=2] {'slab','plane'}, use_global_device_ids=true, to_apply=%region_12.13 | all-reduce | flops 1152 | bytes 9216 | tf_op jit(solution)/shard_map/psum | solution.py:207
  283.4 242.6 %all-reduce.3.cloned.1.call-done = f32[640,64]{0,1:T(8,128)} async-done(((f32[640,64]{0,1:T(8,128)}), f32[640,64]{0,1:T(8,128)}) %all-reduce.3.cloned.1.call-update) | async-done | bytes 163856 | tf_op jit(solution)/shard_map/psum | solution.py:207
  (127 shorter events, 47.4 us)
Async XLA Ops:
  8.0 33.3 %copy-start = (bf16[640,64]{0,1:T(8,128)(2,1)S(1)}, bf16[640,64]{0,1:T(8,128)(2,1)}, u32[]{:S(2)}) copy-start(bf16[640,64]{0,1:T(8,128)(2,1)} %param.15) | copy-start | bytes 245764
  8.0 518.0 %all-reduce.3.cloned.1.call-start = ((), (), s32[]{:S(2)}) async-start(), calls=%async_computation.2 | async-start | bytes 327680 | tf_op jit(solution)/shard_map/psum | solution.py:207
  15.8 8.4 %collective-permute-start = (bf16[131,256]{0,1:T(8,128)(2,1)S(1)}, bf16[131,256]{0,1:T(8,128)(2,1)S(1)}, u32[]{:S(2)}, u32[]{:S(2)}) collective-permute-start(bf16[131,256]{0,1:T(8,128)(2,1)S(1)} %all_gather.3), channel_id=1, source_target_pairs={{0,2},{2,4},{4,6},{6,8},{8,10},{10,12},{12,14},{14,16},{16,18},{18... | collective-permute-start | bytes 201224 | tf_op jit(solution)/shard_map/ppermute | solution.py:17
  18.8 5.5 %collective-permute-start.1 = (bf16[131,256]{0,1:T(8,128)(2,1)S(1)}, bf16[131,256]{0,1:T(8,128)(2,1)S(1)}, u32[]{:S(2)}, u32[]{:S(2)}) collective-permute-start(bf16[131,256]{0,1:T(8,128)(2,1)S(1)} %all_gather.3), channel_id=1, source_target_pairs={{2,0},{4,2},{6,4},{8,6},{10,8},{12,10},{14,12},{16,14},{18,16},{20... | collective-permute-start | bytes 201224 | tf_op jit(solution)/shard_map/ppermute | solution.py:20
  20.9 3.4 copy-start.12
  24.2 16.0 %copy-start.14 = (f32[8]{0:T(128)}, f32[8]{0:T(128)S(1)}, u32[]{:S(2)}) copy-start(f32[8]{0:T(128)S(1)} %iota_multiply_fusion) | copy-start | bytes 100
  36.5 3.8 copy-start.13
  38.5 8.3 %copy-start.10 = (f32[1,4096]{1,0:T(1,128)}, f32[1,4096]{1,0:T(1,128)S(1)}, u32[]{:S(2)}) copy-start(f32[1,4096]{1,0:T(1,128)S(1)} %get-tuple-element.150) | copy-start | bytes 49156
  41.3 5.4 %copy-start.5 = (f32[64,4096]{1,0:T(8,128)}, f32[64,4096]{1,0:T(8,128)S(1)}, u32[]{:S(2)}) copy-start(f32[64,4096]{1,0:T(8,128)S(1)} %convolution_bitcast_fusion.1) | copy-start | bytes 3145732
  101.6 4.9 copy-start.3
  109.6 3.4 copy-start.1
  109.6 3.4 copy-start.8
  113.0 3.2 copy-start.9
  113.0 3.2 copy-start.16
  113.0 3.2 copy-start.17
  113.0 3.2 copy-start.18
  113.0 3.2 copy-start.19
  113.0 3.2 copy-start.20
  157.9 5.4 %copy-start.6 = (f32[64,4096]{1,0:T(8,128)S(1)}, f32[64,4096]{1,0:T(8,128)}, u32[]{:S(2)}) copy-start(f32[64,4096]{1,0:T(8,128)} %copy-done.5) | copy-start | bytes 3145732
  167.9 30.7 %copy-start.11 = (f32[1,4096]{1,0:T(1,128)S(1)}, f32[1,4096]{1,0:T(1,128)}, u32[]{:S(2)}) copy-start(f32[1,4096]{1,0:T(1,128)} %copy-done.10) | copy-start | bytes 49156
  167.9 30.7 %copy-start.15 = (f32[8]{0:T(128)S(1)}, f32[8]{0:T(128)}, u32[]{:S(2)}) copy-start(f32[8]{0:T(128)} %copy-done.14) | copy-start | bytes 100
  192.5 89.7 %collective-permute-start.3 = (f32[128,256]{0,1:T(8,128)S(1)}, f32[128,256]{0,1:T(8,128)S(1)}, u32[]{:S(2)}, u32[]{:S(2)}) collective-permute-start(f32[128,256]{0,1:T(8,128)S(1)} %get-tuple-element.117), channel_id=1, source_target_pairs={{254,0},{0,2},{2,4},{4,6},{6,8},{8,10},{10,12},{12,14},{14,16},{16... | collective-permute-start | bytes 393224 | tf_op jit(solution)/shard_map/ppermute | solution.py:28
  193.7 88.5 %collective-permute-start.2 = (f32[128,256]{0,1:T(8,128)S(1)}, f32[128,256]{0,1:T(8,128)S(1)}, u32[]{:S(2)}, u32[]{:S(2)}) collective-permute-start(f32[128,256]{0,1:T(8,128)S(1)} %get-tuple-element.116), channel_id=1, source_target_pairs={{2,0},{4,2},{6,4},{8,6},{10,8},{12,10},{14,12},{16,14},{18,16},{20... | collective-permute-start | bytes 393224 | tf_op jit(solution)/shard_map/ppermute | solution.py:28
  281.6 246.1 %reduce-scatter.2.cloned.1.call-start = ((), (), s32[]{:S(2)}) async-start(), calls=%async_computation.1 | async-start | bytes 196608 | tf_op jit(solution)/shard_map/reduce_scatter | solution.py:206
  (8 other events, 22.3 us)
Sparse Core Ops, SparseCore 0:
  281.7 244.2 all-reduce.2
Sparse Core Ops, SparseCore 1:
  284.5 12.7 reduce-scatter.1
where the time goes:
time: 544 us; the launch traced here: 537 us
  waiting for transfers between devices  243 us (45%)
  blocking collectives  86.1 us (16%)
  local copies, waits for them, and re-layouts  78.1 us (14%)
  other arithmetic  56.8 us (10%)
  matrix products  47 us (9%)
  between operations  16.3 us (3%)
  starting transfers between devices  9.81 us (2%)
    psum x1, waiting for transfers between devices, shards(): lax.psum((totals[1], totals[2], totals[3]), ('slab', 'plane'))  243 us
    psum x1, blocking collectives, shards(): lax.psum((totals[1], totals[2], totals[3]), ('slab', 'plane'))  80.1 us
    scatter-add x1, other arithmetic, advance(): grad_window = grad_window.at[:, flat_rows].add(grad_features)  24.6 us
    dot_general x5, matrix products, probe_block(): jnp.einsum('kjp,cjp->kcp', part_y, messages[degree], precision=lax.Precis...  19.5 us
    gather x1, local copies, waits for them, and re-layouts, advance(): features = jnp.take(window_feat, flat_rows, axis=1)  14.9 us
    dot_general x4, matrix products, probe_block(): jnp.einsum('kjp,kcp->cjp', part_y, grad_mom, precision=lax.Precision.HIGH...  14.3 us
    gather x2, local copies, waits for them, and re-layouts, advance(): atom_xyz = jnp.take(window_xyz, flat_rows, axis=1).astype(jnp.float32)  12.5 us
    mul x1, local copies, waits for them, and re-layouts, probe_block(): grad_messages * feat_float[None] * weight[None, None, :]  11.3 us
  transfers between devices with their start and end apart: 6, of which 1 were waited for; matrix products, arithmetic and copies ran while one was open for 2% of the time, Pallas kernels for 0%

commit v1 on v0

--- a/solution.py
+++ b/solution.py
@@ -205,7 +205,7 @@
     owned_part = grad_window[:, atom_slab : 2 * atom_slab] + lower_part + upper_part
     grad_feat = lax.psum_scatter(owned_part, "plane", scatter_dimension=1, tiled=True)
     summed_w1, summed_w2, summed_read = lax.psum(
-        (totals[1], totals[2], totals[3]), ("slab", "plane")
+        lax.psum((totals[1], totals[2], totals[3]), "slab"), "plane"
     )
     scale = 1.0 / math.sqrt(probe_dev * slab_count * plane_count)
     return (

time: 544 us -> 1510 us (2.78)
  waiting for transfers between devices: 243 us -> 1000 us
  blocking collectives: 86.1 us -> 296 us
    psum x1 -> x2, waiting for transfers between devices: 243 us -> 984 us  [the longest x1 951 us: shards(): lax.psum((totals[1], totals[2], totals[3]), 'slab')]
    psum x1 -> x2, blocking collectives: 80.1 us -> 290 us  [the longest x1 285 us: shards(): lax.psum((totals[1], totals[2], totals[3]), 'slab')]
    reduce_scatter x1, waiting for transfers between devices: 0.01 us -> 17.6 us  [shards(): lax.psum_scatter(owned_part, 'plane', scatter_dimension=1, tiled=True)]
  transfers between devices with their start and end apart: 6 -> 7, of which waited for: 1 -> 3; matrix products, arithmetic and copies ran while one was open for 2% -> 1% of each run, Pallas kernels for 0% -> 0%
where the time goes in v1:
time: 1510 us; the launch traced here: 1500 us
  waiting for transfers between devices  1000 us (66%)
  blocking collectives  296 us (20%)
  local copies, waits for them, and re-layouts  78.1 us (5%)
  other arithmetic  56.8 us (4%)
  matrix products  47 us (3%)
    psum x1, waiting for transfers between devices, shards(): lax.psum((totals[1], totals[2], totals[3]), 'slab')  951 us
    psum x1, blocking collectives, shards(): lax.psum((totals[1], totals[2], totals[3]), 'slab')  285 us
    psum x1, waiting for transfers between devices, shards(): lax.psum(lax.psum((totals[1], totals[2], totals[3]), 'slab'), 'plane')  32.7 us
  transfers between devices with their start and end apart: 7, of which 3 were waited for; matrix products, arithmetic and copies ran while one was open for 1% of the time, Pallas kernels for 0%

profile of v1, /device:TPU:1, one launch (start us, length us, event | category | flops | bytes accessed | tf_op | source)
XLA Modules:
  0.0 1503.8 jit_solution(13497812239149530609)
XLA Ops:
  8.9 6.0 all_gather.3
  23.5 12.1 gather_fusion
  40.5 5.4 fusion.59
  45.9 11.3 copy.168
  57.2 14.9 gather_fusion.1
  72.1 3.4 convert_bitcast_fusion
  75.4 5.8 multiply_multiply_fusion
  81.3 4.0 fusion.61
  85.3 5.2 fusion.5
  100.8 4.8 multiply_reduce_fusion.1
  116.1 3.5 convolution_bitcast_fusion.5
  120.8 3.9 convolution_bitcast_fusion.4
  125.8 3.5 convolution_bitcast_fusion.3
  130.5 3.5 convolution_bitcast_fusion.2
  138.3 7.6 broadcast_multiply_fusion
  145.8 11.3 copy.186
  157.1 5.4 fusion
  167.0 24.6 %scatter_custom_fusion = f32[128,768]{0,1:T(8,128)S(1)} fusion(s32[4096]{0:T(1024)} %bitcast.154, f32[128,4096]{0,1:T(8,128)S(1)} %copy-done.4, f32[4096]{0:T(1024)S(1)} %multiply_bitcast_fusion.1, f32[]{:T(128)} %constant.170.clone.1), kind=kCustom, calls=%fused_computation.12 | custom fusion | flops 1048576 | bytes 2507264 | tf_op jit(solution)/shard_map/while/body/eval_jaxpr/scatter-add | solution.py:187
  192.9 4.9 collective-permute-start.2
  200.0 284.9 %all-reduce = (f32[64,8]{0,1:T(8,128)S(1)}, f32[5,128]{1,0:T(8,128)S(1)}) all-reduce(f32[64,8]{0,1:T(8,128)S(1)} %fusion.39, f32[5,128]{1,0:T(8,128)S(1)} %stack.121), channel_id=1, replica_groups=mesh['slab'=128,'plane'=2] {'slab'}, use_global_device_ids=true, to_apply=%region_12.13 | all-reduce | flops 1152 | bytes 9216 | tf_op jit(solution)/shard_map/psum | solution.py:208
  484.9 5.3 all-reduce.1
  491.5 950.8 %all-reduce.5.cloned.1.call-done = f32[640,64]{0,1:T(8,128)} async-done(((f32[640,64]{0,1:T(8,128)}), f32[640,64]{0,1:T(8,128)}) %all-reduce.5.cloned.1.call-update) | async-done | bytes 163856 | tf_op jit(solution)/shard_map/psum | solution.py:208
  1443.6 32.7 %all-reduce.7.cloned.1.call-done = f32[640,64]{0,1:T(8,128)} async-done(((f32[640,64]{0,1:T(8,128)}), f32[640,64]{0,1:T(8,128)}) %all-reduce.7.cloned.1.call-update) | async-done | bytes 163856 | tf_op jit(solution)/shard_map/psum | solution.py:207
  1477.9 17.6 %reduce-scatter.2.cloned.1.call-done = f32[128,128]{0,1:T(8,128)} async-done(((f32[128,256]{0,1:T(8,128)}), f32[128,128]{0,1:T(8,128)}) %reduce-scatter.2.cloned.1.call-update) | async-done | bytes 65552 | tf_op jit(solution)/shard_map/reduce_scatter | solution.py:206
  (131 shorter events, 57.0 us)
Async XLA Ops:
  7.2 33.3 %copy-start = (bf16[640,64]{0,1:T(8,128)(2,1)S(1)}, bf16[640,64]{0,1:T(8,128)(2,1)}, u32[]{:S(2)}) copy-start(bf16[640,64]{0,1:T(8,128)(2,1)} %param.15) | copy-start | bytes 245764
  7.2 1435.1 %all-reduce.5.cloned.1.call-start = ((), (), s32[]{:S(2)}) async-start(), calls=%async_computation.2 | async-start | bytes 327680 | tf_op jit(solution)/shard_map/psum | solution.py:208
  15.0 8.4 collective-permute-start
  18.0 5.5 collective-permute-start.1
  20.0 3.4 copy-start.12
  23.4 16.0 %copy-start.14 = (f32[8]{0:T(128)}, f32[8]{0:T(128)S(1)}, u32[]{:S(2)}) copy-start(f32[8]{0:T(128)S(1)} %iota_multiply_fusion) | copy-start | bytes 100
  35.7 3.8 copy-start.13
  37.7 8.3 copy-start.10
  40.5 5.4 copy-start.5
  100.8 4.9 copy-start.3
  108.8 3.4 copy-start.1
  108.8 3.4 copy-start.8
  112.1 3.2 copy-start.9
  112.2 3.2 copy-start.16
  112.2 3.2 copy-start.17
  112.2 3.2 copy-start.18
  112.2 3.2 copy-start.19
  157.1 5.4 copy-start.6
  167.0 30.7 %copy-start.11 = (f32[1,4096]{1,0:T(1,128)S(1)}, f32[1,4096]{1,0:T(1,128)}, u32[]{:S(2)}) copy-start(f32[1,4096]{1,0:T(1,128)} %copy-done.10) | copy-start | bytes 49156
  167.0 30.7 %copy-start.15 = (f32[8]{0:T(128)S(1)}, f32[8]{0:T(128)}, u32[]{:S(2)}) copy-start(f32[8]{0:T(128)} %copy-done.14) | copy-start | bytes 100
  191.7 1250.7 %collective-permute-start.3 = (f32[128,256]{0,1:T(8,128)S(1)}, f32[128,256]{0,1:T(8,128)S(1)}, u32[]{:S(2)}, u32[]{:S(2)}) collective-permute-start(f32[128,256]{0,1:T(8,128)S(1)} %get-tuple-element.119), channel_id=1, source_target_pairs={{254,0},{0,2},{2,4},{4,6},{6,8},{8,10},{10,12},{12,14},{14,16},{16... | collective-permute-start | bytes 393224 | tf_op jit(solution)/shard_map/ppermute | solution.py:28
  192.9 1249.5 %collective-permute-start.2 = (f32[128,256]{0,1:T(8,128)S(1)}, f32[128,256]{0,1:T(8,128)S(1)}, u32[]{:S(2)}, u32[]{:S(2)}) collective-permute-start(f32[128,256]{0,1:T(8,128)S(1)} %get-tuple-element.118), channel_id=1, source_target_pairs={{2,0},{4,2},{6,4},{8,6},{10,8},{12,10},{14,12},{16,14},{18,16},{20... | collective-permute-start | bytes 393224 | tf_op jit(solution)/shard_map/ppermute | solution.py:28
  490.9 985.5 %all-reduce.7.cloned.1.call-start = ((), (), s32[]{:S(2)}) async-start(), calls=%async_computation.3 | async-start | bytes 327680 | tf_op jit(solution)/shard_map/psum | solution.py:207
  1442.3 53.2 %reduce-scatter.2.cloned.1.call-start = ((), (), s32[]{:S(2)}) async-start(), calls=%async_computation.1 | async-start | bytes 196608 | tf_op jit(solution)/shard_map/reduce_scatter | solution.py:206
  (9 other events, 25.5 us)
Sparse Core Ops, SparseCore 0:
  491.0 951.2 all-reduce.4
  1444.8 31.4 all-reduce.6
  1478.8 16.6 reduce-scatter.1
